TPU v7x, 32 devices: a whole 2x2x4 slice. The times are simulated.
32 devices in a mesh: gx: 8 (over z, core), gy: 2 (over x), ga: 2 (over y).
Axes of the slice: x: 2, y: 2, z: 4, core: 2. Of those that a mesh axis runs over, the one named last changes fastest.
Arguments:
- euler_table: float32 [3, 2048], replicated, may hold values from -3.140625 to 3.140625
- crystal: float32 [21], replicated, may hold values from -0.08 to 3.4
- orient: int32 [32, 8, 2, 512], P('ga', 'gx', 'gy'), may hold values from 0 to 2047
- weight: bfloat16 [32, 8, 2, 512], P('ga', 'gx', 'gy'), may hold values from 0.099609375 to 1
- cell_map: int32 [8, 2, 512], P('gx', 'gy'), may hold values from 0 to 511, each once within a row
- density: float32 [64, 8, 16], P('gx', 'gy', 'ga'), may hold values from 0.5 to 2
- velocity: float32 [3, 64, 8, 16], P(None, 'gx', 'gy', 'ga'), may hold values from -6 to 6
- stress: float32 [6, 64, 8, 16], P(None, 'gx', 'gy', 'ga'), may hold values from -6 to 6
Outputs:
- stiffness: float32 [21, 64, 8, 16], P(None, 'gx', 'gy', 'ga')
- final_velocity: float32 [3, 64, 8, 16], P(None, 'gx', 'gy', 'ga')
- final_stress: float32 [6, 64, 8, 16], P(None, 'gx', 'gy', 'ga')
Inputs may be any that keep to these rules, and one draw needn't show every extreme that they name: `cell_map`: each partition's row is a permutation of the 512 canonical indices.
All inputs are finite; a program needn't handle non-finite values.
Results may differ from a plain program's by a relative error of at most 0.0003.
Values sent between devices are 32-bit elements; how exact they have to be, the bound alone decides.
No kernel may reach another device: no remote copies, remote signals or barrier semaphores. Data moves between devices by JAX's collectives and lax.ppermute only.
A program may use at most 128 MiB of HBM per device.

v0:
```python
import jax
import jax.numpy as jnp
from jax import lax
from jax.sharding import PartitionSpec as P

STEPS = 2
stencil_weights = (0.8, -0.2, 4.0 / 105.0, -1.0 / 280.0)
time_step = 0.2
grain_block = 4
voigt_pairs = ((0, 0), (1, 1), (2, 2), (1, 2), (0, 2), (0, 1))
upper_pairs = [
    (row_index, col_index) for row_index in range(6) for col_index in range(row_index, 6)
]


def with_halo(cells, sides, width):
    for axis, dim in sides:
        count = lax.axis_size(axis)
        ends = count - 1
        head = lax.slice_in_dim(cells, 0, width, axis=dim)
        tail = lax.slice_in_dim(cells, cells.shape[dim] - width, cells.shape[dim], axis=dim)
        cells = jnp.concatenate(
            [
                lax.ppermute(tail, axis, [(i, (i + 1) % count) for i in range(ends)]),
                cells,
                lax.ppermute(head, axis, [((i + 1) % count, i) for i in range(ends)]),
            ],
            axis=dim,
        )
    return cells


def symmetric_index(first_index, second_index):
    return upper_pairs.index((min(first_index, second_index), max(first_index, second_index)))


def ordered_sum(summands):
    running = summands[0]
    for summand in summands[1:]:
        running = running + summand
    return running


def rotated_table(euler_table, crystal):
    cos_one, sin_one = (jnp.cos(euler_table[0]), jnp.sin(euler_table[0]))
    cos_mid, sin_mid = (jnp.cos(euler_table[1]), jnp.sin(euler_table[1]))
    cos_two, sin_two = (jnp.cos(euler_table[2]), jnp.sin(euler_table[2]))
    bunge = [
        [
            cos_one * cos_two - sin_one * sin_two * cos_mid,
            sin_one * cos_two + cos_one * sin_two * cos_mid,
            sin_two * sin_mid,
        ],
        [
            -cos_one * sin_two - sin_one * cos_two * cos_mid,
            -sin_one * sin_two + cos_one * cos_two * cos_mid,
            cos_two * sin_mid,
        ],
        [sin_one * sin_mid, -cos_one * sin_mid, cos_mid],
    ]
    rotation = [[bunge[col_index][row_index] for col_index in range(3)] for row_index in range(3)]
    bond = []
    for out_index in range(6):
        first, second = voigt_pairs[out_index]
        bond_row = []
        for in_index in range(6):
            third, fourth = voigt_pairs[in_index]
            if in_index < 3:
                bond_row.append(rotation[first][third] * rotation[second][third])
            else:
                bond_row.append(
                    rotation[first][third] * rotation[second][fourth]
                    + rotation[first][fourth] * rotation[second][third]
                )
        bond.append(bond_row)
    entries = [
        [crystal[symmetric_index(row_index, col_index)] for col_index in range(6)]
        for row_index in range(6)
    ]
    product = [
        [
            ordered_sum([bond[row_index][inner] * entries[inner][col_index] for inner in range(6)])
            for col_index in range(6)
        ]
        for row_index in range(6)
    ]
    rotated = [
        ordered_sum([product[row_index][inner] * bond[col_index][inner] for inner in range(6)])
        for row_index, col_index in upper_pairs
    ]
    return jnp.stack(rotated)


def accumulate(table, orient_rows, weight_rows):
    blocks = orient_rows.shape[0] // grain_block
    count_cells = orient_rows.shape[1]

    def absorb(carry, inputs):
        chosen, masses = inputs
        picked = jnp.take(table, chosen, axis=1)
        masses_wide = masses.astype(jnp.float32)
        return (
            (
                carry[0] + jnp.sum(picked * masses_wide[None], axis=1),
                carry[1] + jnp.sum(masses_wide, axis=0),
            ),
            None,
        )

    initial = (jnp.zeros((21, count_cells), jnp.float32), jnp.zeros((count_cells,), jnp.float32))
    result, unused = lax.scan(
        absorb,
        initial,
        (
            orient_rows.reshape(blocks, grain_block, count_cells),
            weight_rows.reshape(blocks, grain_block, count_cells),
        ),
    )
    return result


def derivative(padded, direction):
    interior = [padded.shape[0]] + [extent - 8 for extent in padded.shape[1:]]

    def window(offset):
        starts = [0, 4, 4, 4]
        starts[direction] = 4 + offset
        return lax.slice(
            padded, starts, [begin + extent for begin, extent in zip(starts, interior)]
        )

    result = stencil_weights[0] * (window(1) - window(-1))
    for order_index in range(1, 4):
        result = result + stencil_weights[order_index] * (
            window(order_index + 1) - window(-order_index - 1)
        )
    return result


def advance_velocity(velocity, padded_stress, density):
    along_x = derivative(jnp.stack([padded_stress[0], padded_stress[5], padded_stress[4]]), 1)
    along_y = derivative(jnp.stack([padded_stress[5], padded_stress[1], padded_stress[3]]), 2)
    along_z = derivative(jnp.stack([padded_stress[4], padded_stress[3], padded_stress[2]]), 3)
    return velocity + time_step * (along_x + along_y + along_z) / density[None]


def advance_stress(stress, padded_velocity, stiffness):
    grad_x = derivative(padded_velocity, 1)
    grad_y = derivative(padded_velocity, 2)
    grad_z = derivative(padded_velocity, 3)
    strain = [
        grad_x[0],
        grad_y[1],
        grad_z[2],
        grad_y[2] + grad_z[1],
        grad_x[2] + grad_z[0],
        grad_x[1] + grad_y[0],
    ]
    updated = []
    for row_index in range(6):
        change = ordered_sum(
            [
                stiffness[symmetric_index(row_index, col_index)] * strain[col_index]
                for col_index in range(6)
            ]
        )
        updated.append(stress[row_index] + time_step * change)
    return jnp.stack(updated)


def on_device(euler_table, crystal, orient, weight, cell_map, density, velocity, stress):
    part_x = lax.axis_size("gx")
    part_y = lax.axis_size("gy")
    layers = lax.axis_size("ga")
    brick_x, brick_y, brick_z = (stress.shape[1], stress.shape[2], stress.shape[3])
    sub_x = brick_x // part_x
    sub_y = brick_y // part_y
    depth = brick_z * layers
    grains = orient.shape[0]
    count_cells = orient.shape[3]
    table = rotated_table(euler_table, crystal)
    summed, total = accumulate(
        table, orient.reshape(grains, count_cells), weight.reshape(grains, count_cells)
    )
    slots = cell_map.reshape(count_cells)
    layer_pos = slots % depth
    remainder = slots // depth
    sub_y_pos = remainder % sub_y
    remainder = remainder // sub_y
    brick_y_pos = remainder % part_y
    remainder = remainder // part_y
    sub_x_pos = remainder % sub_x
    brick_x_pos = remainder // sub_x
    target = (
        ((brick_x_pos * part_y + brick_y_pos) * sub_x + sub_x_pos) * sub_y + sub_y_pos
    ) * depth + layer_pos
    placed = jnp.zeros((21, count_cells), jnp.float32).at[:, target].set(summed)
    counted = jnp.zeros((count_cells,), jnp.float32).at[target].set(total)
    placed = placed.reshape(21, part_x * part_y, sub_x, sub_y, depth)
    counted = counted.reshape(part_x * part_y, sub_x, sub_y, depth)
    placed, counted = (
        lax.psum_scatter(placed, "ga", scatter_dimension=4, tiled=True),
        lax.psum_scatter(counted, "ga", scatter_dimension=3, tiled=True),
    )
    averaged = placed / counted[None]
    moved = lax.all_to_all(averaged, ("gx", "gy"), split_axis=1, concat_axis=1, tiled=True)
    moved = moved.reshape(21, part_x, part_y, sub_x, sub_y, brick_z)
    stiffness = moved.transpose(0, 1, 3, 2, 4, 5).reshape(21, brick_x, brick_y, brick_z)
    for step_index in range(STEPS):
        padded_stress = with_halo(stress, (("gx", 1), ("gy", 2), ("ga", 3)), 4)
        velocity = advance_velocity(velocity, padded_stress, density)
        padded_velocity = with_halo(velocity, (("gx", 1), ("gy", 2), ("ga", 3)), 4)
        stress = advance_stress(stress, padded_velocity, stiffness)
    return (stiffness, velocity, stress)


def solution(mesh):
    return jax.shard_map(
        on_device,
        mesh=mesh,
        in_specs=(
            P(),
            P(),
            P("ga", "gx", "gy", None),
            P("ga", "gx", "gy", None),
            P("gx", "gy", None),
            P("gx", "gy", "ga"),
            P(None, "gx", "gy", "ga"),
            P(None, "gx", "gy", "ga"),
        ),
        out_specs=(P(None, "gx", "gy", "ga"), P(None, "gx", "gy", "ga"), P(None, "gx", "gy", "ga")),
        check_vma=False,
    )
```

profile of v0, /device:TPU:6, one launch (start us, length us, event | category | flops | bytes accessed | tf_op | source)
XLA Modules:
  0.0 305.0 jit_solution(5697528187163204053)
XLA Ops:
  7.2 1.0 copy.84
  8.3 1.7 collective-permute-start
  10.0 1.3 collective-permute-start.1
  12.7 0.8 copy-done.4
  13.4 14.0 %multiply_add_fusion.6 = (f32[1,2048]{1,0:T(1,128)S(1)}, f32[1,2048]{1,0:T(1,128)S(1)}, f32[1,2048]{1,0:T(1,128)S(1)}, f32[1,2048]{1,0:T(1,128)S(1)}, f32[1,2048...) fusion(f32[]{:T(128)} %bitcast.22, f32[]{:T(128)} %bitcast.21, ...), kind=kLoop, calls=%fused_computation.295 | loop fusion | flops 219136 | bytes 131156 | tf_op jit(solution)/shard_map/add | solution.py:40
  27.5 13.8 %multiply_add_fusion.7 = (f32[1,2048]{1,0:T(1,128)S(1)}, f32[1,2048]{1,0:T(1,128)S(1)}, f32[1,2048]{1,0:T(1,128)S(1)}, f32[1,2048]{1,0:T(1,128)S(1)}, f32[1,2048...) fusion(f32[1,2048]{1,0:T(1,128)S(1)} %get-tuple-element.135, ...), kind=kLoop, calls=%fused_computation.296 | loop fusion | flops 186368 | bytes 163924 | tf_op jit(solution)/shard_map/add | solution.py:40
  41.3 13.3 %multiply_add_fusion.34 = (f32[1,2048]{1,0:T(1,128)S(1)}, f32[1,2048]{1,0:T(1,128)S(1)}, f32[1,2048]{1,0:T(1,128)S(1)}, f32[1,2048]{1,0:T(1,128)S(1)}, f32[1,204...) fusion(f32[1,2048]{1,0:T(1,128)S(1)} %get-tuple-element.135, ...), kind=kLoop, calls=%fused_computation.323 | loop fusion | flops 174080 | bytes 155732 | tf_op jit(solution)/shard_map/add | solution.py:40
  54.6 13.5 %multiply_add_fusion.15 = (f32[1,2048]{1,0:T(1,128)S(1)}, f32[1,2048]{1,0:T(1,128)S(1)}, f32[1,2048]{1,0:T(1,128)S(1)}, f32[1,2048]{1,0:T(1,128)S(1)}, f32[1,204...) fusion(f32[1,2048]{1,0:T(1,128)S(1)} %get-tuple-element.135, f32[1,2048]{1,0:T(1,128)S(1)} %get-tuple-element.134, ...), kind=kLoop, calls=%fused_computation.304 | loop fusion | flops 182272 | bytes 155732 | tf_op jit(solution)/shard_map/add | solution.py:40
  68.1 13.5 %multiply_add_fusion.24 = (f32[1,2048]{1,0:T(1,128)S(1)}, f32[1,2048]{1,0:T(1,128)S(1)}, f32[1,2048]{1,0:T(1,128)S(1)}, f32[1,2048]{1,0:T(1,128)S(1)}, f32[1,204...) fusion(f32[1,2048]{1,0:T(1,128)S(1)} %get-tuple-element.135, ...), kind=kLoop, calls=%fused_computation.313 | loop fusion | flops 174080 | bytes 139348 | tf_op jit(solution)/shard_map/add | solution.py:40
  81.7 13.3 %multiply_add_fusion.8 = f32[1,2048]{1,0:T(1,128)S(1)} fusion(f32[1,2048]{1,0:T(1,128)S(1)} %get-tuple-element.148, f32[1,2048]{1,0:T(1,128)S(1)} %get-tuple-element.147, f32[1,2048]{1,0:T(1,128)S(1)} %get-tuple-element.146, f32[1,2048]{1,0:T(1,128)S(1)} %get-tuple-element.145, f32[1,2048]{1,0:T(1,128)S(1)} %get-tuple-element.144, ...), kind=kLoop, calls=%fused_computation.297 | loop fusion | flops 157696 | bytes 57428 | tf_op jit(solution)/shard_map/add | solution.py:40
  95.0 13.3 %multiply_add_fusion.16 = f32[1,2048]{1,0:T(1,128)S(1)} fusion(f32[1,2048]{1,0:T(1,128)S(1)} %get-tuple-element.148, f32[1,2048]{1,0:T(1,128)S(1)} %get-tuple-element.147, f32[1,2048]{1,0:T(1,128)S(1)} %get-tuple-element.146, f32[1,2048]{1,0:T(1,128)S(1)} %get-tuple-element.145, f32[1,2048]{1,0:T(1,128)S(1)} %get-tuple-element.144, ...), kind=kLoop, calls=%fused_computation.305 | loop fusion | flops 157696 | bytes 106580 | tf_op jit(solution)/shard_map/add | solution.py:40
  108.4 13.3 %multiply_add_fusion.45 = (f32[1,2048]{1,0:T(1,128)S(1)}, f32[1,2048]{1,0:T(1,128)S(1)}, f32[1,2048]{1,0:T(1,128)S(1)}, f32[1,2048]{1,0:T(1,128)S(1)}, f32[1,204...) fusion(f32[1,2048]{1,0:T(1,128)S(1)} %get-tuple-element.135, ...), kind=kLoop, calls=%fused_computation.334 | loop fusion | flops 174080 | bytes 155732 | tf_op jit(solution)/shard_map/add | solution.py:40
  122.5 13.3 %multiply_add_fusion.17 = f32[1,2048]{1,0:T(1,128)S(1)} fusion(f32[1,2048]{1,0:T(1,128)S(1)} %get-tuple-element.157, f32[1,2048]{1,0:T(1,128)S(1)} %get-tuple-element.156, f32[1,2048]{1,0:T(1,128)S(1)} %get-tuple-element.155, f32[1,2048]{1,0:T(1,128)S(1)} %get-tuple-element.154, f32[1,2048]{1,0:T(1,128)S(1)} %get-tuple-element.153, ...), kind=kLoop, calls=%fused_computation.306 | loop fusion | flops 157696 | bytes 57428 | tf_op jit(solution)/shard_map/add | solution.py:40
  137.8 1.3 collective-permute-start.2
  139.1 4.6 %collective-permute-start.3 = (f32[6,16,4,8]{1,3,2,0:T(8,128)S(1)}, f32[6,16,4,8]{1,3,2,0:T(8,128)S(1)}, u32[]{:S(2)}, u32[]{:S(2)}) collective-permute-start(f32[6,16,4,8]{1,3,2,0:T(8,128)S(1)} %pad_maximum_fusion.13), channel_id=1, source_target_pairs={{2,0},{3,1},{6,4},{7,5},{10,8},{11,9},{14,12},{15,13},{18,16},{19,... | collective-permute-start | bytes 36872 | tf_op jit(solution)/shard_map/ppermute | solution.py:26
  143.7 25.7 %while.13 = (s32[]{:T(128)}, f32[21,512]{0,1:T(8,128)S(1)}, f32[512]{0:T(512)S(1)}, s32[4,4,512]{2,1,0:T(4,128)S(1)}, f32[21,2048]{0,1:T(8,128)S(1)}, /*index=5*/bf16[4,4,512]{2,1,0:T(4,128)(2,1)S(1)}, s32[]{:T(128)}, s32[]{:T(128)}) while((s32[]{:T(128)}, f32[21,512]{0,1:T(8,128)S(1)}, f32[512]{0:T(512)S(1)}, ...), condition=%wide.region_3.4_spmd.clone, body=%wide.region_0.3_spmd.clone.sunk | while | flops 166915 | bytes 790640 | solution.py:111
  143.7 5.5 %gather_fusion = f32[2048,21]{1,0:T(8,128)S(1)} fusion(f32[21,2048]{0,1:T(8,128)S(1)} %get-tuple-element.310, s32[2048]{0:T(1024)S(1)} %broadcast_clamp_fusion.2), kind=kCustom, calls=%fused_computation.clone.clone.1 | custom fusion | bytes 352256 | tf_op jit(solution)/shard_map/while/body/eval_jaxpr/jit(_take)/gather | solution.py:100
  150.1 5.5 %gather_fusion = f32[2048,21]{1,0:T(8,128)S(1)} fusion(f32[21,2048]{0,1:T(8,128)S(1)} %get-tuple-element.310, s32[2048]{0:T(1024)S(1)} %broadcast_clamp_fusion.2), kind=kCustom, calls=%fused_computation.clone.clone.1 | custom fusion | bytes 352256 | tf_op jit(solution)/shard_map/while/body/eval_jaxpr/jit(_take)/gather | solution.py:100
  156.6 5.5 %gather_fusion = f32[2048,21]{1,0:T(8,128)S(1)} fusion(f32[21,2048]{0,1:T(8,128)S(1)} %get-tuple-element.310, s32[2048]{0:T(1024)S(1)} %broadcast_clamp_fusion.2), kind=kCustom, calls=%fused_computation.clone.clone.1 | custom fusion | bytes 352256 | tf_op jit(solution)/shard_map/while/body/eval_jaxpr/jit(_take)/gather | solution.py:100
  163.0 5.5 %gather_fusion = f32[2048,21]{1,0:T(8,128)S(1)} fusion(f32[21,2048]{0,1:T(8,128)S(1)} %get-tuple-element.310, s32[2048]{0:T(1024)S(1)} %broadcast_clamp_fusion.2), kind=kCustom, calls=%fused_computation.clone.clone.1 | custom fusion | bytes 352256 | tf_op jit(solution)/shard_map/while/body/eval_jaxpr/jit(_take)/gather | solution.py:100
  169.6 1.3 collective-permute-start.4
  170.9 4.6 %collective-permute-start.5 = (f32[6,16,12,4]{1,3,2,0:T(4,128)S(1)}, f32[6,16,12,4]{1,3,2,0:T(4,128)S(1)}, u32[]{:S(2)}, u32[]{:S(2)}) collective-permute-start(f32[6,16,12,4]{1,3,2,0:T(4,128)S(1)} %get-tuple-element.205), channel_id=1, source_target_pairs={{1,0},{3,2},{5,4},{7,6},{9,8},{11,10},{13,12},{15,14},{17,16},{19,... | collective-permute-start | bytes 55304 | tf_op jit(solution)/shard_map/ppermute | solution.py:26
  175.5 1.8 scatter_custom_fusion
  177.3 0.8 copy.81
  178.2 2.4 scatter_custom_fusion.1
  182.7 6.7 %all-reduce = f32[16,1,2,16]{0,2,1,3:T(2,128)S(1)} all-reduce(f32[16,1,2,16]{0,2,1,3:T(2,128)S(1)} %copy.82), channel_id=3, replica_groups=mesh['gx'=8,'gy'=2,'ga'=2] {'ga'}, use_global_device_ids=true, to_apply=%region_7.8.clone | all-reduce | flops 512 | bytes 4096
  193.0 1.3 collective-permute-start.6
  194.3 3.0 collective-permute-start.7
  197.3 0.8 collective-permute-done.7
  198.2 1.3 collective-permute-start.8
  199.5 1.3 collective-permute-start.9
  200.8 0.8 collective-permute-done.8
  201.7 4.3 %collective-permute-done.9 = f32[3,16,4,8]{3,2,1,0:T(4,128)S(1)} collective-permute-done((f32[3,16,4,8]{3,2,1,0:T(4,128)S(1)}, f32[3,16,4,8]{3,2,1,0:T(4,128)S(1)}, u32[]{:S(2)}, u32[]{:S(2)}) %collective-permute-start.9) | collective-permute-done | bytes 6176 | tf_op jit(solution)/shard_map/ppermute | solution.py:24
  206.2 3.9 %collective-permute-start.10 = (f32[3,16,12,4]{3,2,1,0:T(8,128)S(1)}, f32[3,16,12,4]{3,2,1,0:T(8,128)S(1)}, u32[]{:S(2)}, u32[]{:S(2)}) collective-permute-start(f32[3,16,12,4]{3,2,1,0:T(8,128)S(1)} %get-tuple-element.202), channel_id=1, source_target_pairs={{1,0},{3,2},{5,4},{7,6},{9,8},{11,10},{13,12},{15,14},{17,16},{19,... | collective-permute-start | bytes 27656 | tf_op jit(solution)/shard_map/ppermute | solution.py:26
  210.1 1.3 collective-permute-start.11
  211.6 1.0 broadcast_divide_fusion
  212.7 0.7 reshape.481
  213.5 11.0 %all-to-all-start = ((f32[16,1,336]{2,1,0:T(1,128)}), f32[16,1,336]{2,1,0:T(1,128)S(1)}, u32[]{:S(2)}, u32[]{:S(2)}) async-start(f32[16,1,336]{2,1,0:T(1,128)} %reshape.481), calls=%async_computation.1 | async-start | bytes 49152 | tf_op jit(solution)/shard_map/all_to_all | solution.py:206
  224.5 0.9 fusion.78
  225.3 4.2 %all-to-all-done = f32[16,1,336]{2,1,0:T(1,128)S(1)} async-done(((f32[16,1,336]{2,1,0:T(1,128)}), f32[16,1,336]{2,1,0:T(1,128)S(1)}, u32[]{:S(2)}, u32[]{:S(2)}) %all-to-all-start) | async-done | bytes 21536 | tf_op jit(solution)/shard_map/all_to_all | solution.py:206
  230.9 1.7 slice_reduce_fusion
  233.8 2.0 collective-permute-start.12
  235.8 1.3 collective-permute-start.13
  237.1 1.9 collective-permute-done.13
  239.1 1.3 collective-permute-start.14
  240.4 4.6 %collective-permute-start.15 = (f32[6,16,4,8]{3,2,1,0:T(4,128)S(1)}, f32[6,16,4,8]{3,2,1,0:T(4,128)S(1)}, u32[]{:S(2)}, u32[]{:S(2)}) collective-permute-start(f32[6,16,4,8]{3,2,1,0:T(4,128)S(1)} %pad_maximum_fusion.12), channel_id=1, source_target_pairs={{2,0},{3,1},{6,4},{7,5},{10,8},{11,9},{14,12},{15,13},{18,16},{19,... | collective-permute-start | bytes 36872 | tf_op jit(solution)/shard_map/ppermute | solution.py:26
  245.0 2.0 collective-permute-done.14
  246.9 1.7 collective-permute-done.15
  249.7 1.3 collective-permute-start.16
  251.5 4.6 %collective-permute-start.17 = (f32[6,16,12,4]{1,3,2,0:T(4,128)S(1)}, f32[6,16,12,4]{1,3,2,0:T(4,128)S(1)}, u32[]{:S(2)}, u32[]{:S(2)}) collective-permute-start(f32[6,16,12,4]{1,3,2,0:T(4,128)S(1)} %copy.91), channel_id=1, source_target_pairs={{1,0},{3,2},{5,4},{7,6},{9,8},{11,10},{13,12},{15,14},{17,16},{19,... | collective-permute-start | bytes 55304 | tf_op jit(solution)/shard_map/ppermute | solution.py:26
  256.1 1.3 collective-permute-done.16
  257.9 1.7 collective-permute-done.17
  261.7 1.3 collective-permute-start.18
  263.0 3.3 %collective-permute-start.19 = (f32[3,4,4,8]{3,2,1,0:T(4,128)S(1)}, f32[3,4,4,8]{3,2,1,0:T(4,128)S(1)}, u32[]{:S(2)}, u32[]{:S(2)}) collective-permute-start(f32[3,4,4,8]{3,2,1,0:T(4,128)S(1)} %get-tuple-element.218), channel_id=1, source_target_pairs={{0,4},{4,8},{8,12},{12,16},{16,20},{20,24},{24,28},{1,5},{5,9},{9,... | collective-permute-start | bytes 4616 | tf_op jit(solution)/shard_map/ppermute | solution.py:24
  266.3 0.8 collective-permute-done.19
  267.2 4.4 %collective-permute-start.20 = (f32[3,16,4,8]{3,2,1,0:T(4,128)S(1)}, f32[3,16,4,8]{3,2,1,0:T(4,128)S(1)}, u32[]{:S(2)}, u32[]{:S(2)}) collective-permute-start(f32[3,16,4,8]{3,2,1,0:T(4,128)S(1)} %pad_maximum_fusion.15), channel_id=1, source_target_pairs={{2,0},{3,1},{6,4},{7,5},{10,8},{11,9},{14,12},{15,13},{18,16},{19,... | collective-permute-start | bytes 18440 | tf_op jit(solution)/shard_map/ppermute | solution.py:26
  271.6 1.3 collective-permute-start.21
  272.9 0.8 collective-permute-done.20
  273.8 4.3 %collective-permute-done.21 = f32[3,16,4,8]{3,2,1,0:T(4,128)S(1)} collective-permute-done((f32[3,16,4,8]{3,2,1,0:T(4,128)S(1)}, f32[3,16,4,8]{3,2,1,0:T(4,128)S(1)}, u32[]{:S(2)}, u32[]{:S(2)}) %collective-permute-start.21) | collective-permute-done | bytes 6176 | tf_op jit(solution)/shard_map/ppermute | solution.py:24
  278.4 4.4 %collective-permute-start.22 = (f32[3,16,12,4]{3,2,1,0:T(8,128)S(1)}, f32[3,16,12,4]{3,2,1,0:T(8,128)S(1)}, u32[]{:S(2)}, u32[]{:S(2)}) collective-permute-start(f32[3,16,12,4]{3,2,1,0:T(8,128)S(1)} %get-tuple-element.200), channel_id=1, source_target_pairs={{1,0},{3,2},{5,4},{7,6},{9,8},{11,10},{13,12},{15,14},{17,16},{19,... | collective-permute-start | bytes 27656 | tf_op jit(solution)/shard_map/ppermute | solution.py:26
  282.8 1.3 collective-permute-start.23
  284.2 8.0 %collective-permute-done.22 = f32[3,16,12,4]{3,2,1,0:T(8,128)S(1)} collective-permute-done((f32[3,16,12,4]{3,2,1,0:T(8,128)S(1)}, f32[3,16,12,4]{3,2,1,0:T(8,128)S(1)}, u32[]{:S(2)}, u32[]{:S(2)}) %collective-permute-start.22) | collective-permute-done | bytes 9248 | tf_op jit(solution)/shard_map/ppermute | solution.py:26
  292.2 4.1 %collective-permute-done.23 = f32[3,16,12,4]{3,2,1,0:T(8,128)S(1)} collective-permute-done((f32[3,16,12,4]{3,2,1,0:T(8,128)S(1)}, f32[3,16,12,4]{3,2,1,0:T(8,128)S(1)}, u32[]{:S(2)}, u32[]{:S(2)}) %collective-permute-start.23) | collective-permute-done | bytes 9248 | tf_op jit(solution)/shard_map/ppermute | solution.py:24
  296.4 0.9 fusion.36
  (145 shorter events, 21.5 us)
Async XLA Ops:
  7.2 204.5 %reduce-scatter.2.cloned.1.call-start = ((), (), s32[]{:S(2)}) async-start(), calls=%async_computation.2 | async-start | bytes 393216 | tf_op jit(solution)/shard_map/reduce_scatter | solution.py:202
  8.3 3.1 %copy-start.3 = (f32[21]{0:T(128)S(1)}, f32[21]{0:T(128)}, u32[]{:S(2)}) copy-start(f32[21]{0:T(128)} %param.11) | copy-start | bytes 256
  8.3 129.4 %collective-permute-start = (f32[6,4,4,8]{1,3,2,0:T(8,128)S(1)}, f32[6,4,4,8]{1,3,2,0:T(8,128)S(1)}, u32[]{:S(2)}, u32[]{:S(2)}) collective-permute-start(f32[6,4,4,8]{1,3,2,0:T(8,128)S(1)} %get-tuple-element.214), channel_id=1, source_target_pairs={{0,4},{4,8},{8,12},{12,16},{16,20},{20,24},{24,28},{1,5},{5,9},{9,... | collective-permute-start | bytes 9224 | tf_op jit(solution)/shard_map/ppermute | solution.py:24
  10.0 127.6 %collective-permute-start.1 = (f32[6,4,4,8]{1,3,2,0:T(8,128)S(1)}, f32[6,4,4,8]{1,3,2,0:T(8,128)S(1)}, u32[]{:S(2)}, u32[]{:S(2)}) collective-permute-start(f32[6,4,4,8]{1,3,2,0:T(8,128)S(1)} %get-tuple-element.215), channel_id=1, source_target_pairs={{4,0},{8,4},{12,8},{16,12},{20,16},{24,20},{28,24},{5,1},{9,5},{13... | collective-permute-start | bytes 9224 | tf_op jit(solution)/shard_map/ppermute | solution.py:26
  12.7 0.8 copy-start.4
  136.1 0.8 copy-start.7
  136.9 0.7 copy-start.8
  137.8 31.6 %collective-permute-start.2 = (f32[6,16,4,8]{1,3,2,0:T(8,128)S(1)}, f32[6,16,4,8]{1,3,2,0:T(8,128)S(1)}, u32[]{:S(2)}, u32[]{:S(2)}) collective-permute-start(f32[6,16,4,8]{1,3,2,0:T(8,128)S(1)} %pad_maximum_fusion.13), channel_id=1, source_target_pairs={{0,2},{1,3},{4,6},{5,7},{8,10},{9,11},{12,14},{13,15},{16,18},{17,... | collective-permute-start | bytes 36872 | tf_op jit(solution)/shard_map/ppermute | solution.py:24
  139.1 30.3 %collective-permute-start.3 = (f32[6,16,4,8]{1,3,2,0:T(8,128)S(1)}, f32[6,16,4,8]{1,3,2,0:T(8,128)S(1)}, u32[]{:S(2)}, u32[]{:S(2)}) collective-permute-start(f32[6,16,4,8]{1,3,2,0:T(8,128)S(1)} %pad_maximum_fusion.13), channel_id=1, source_target_pairs={{2,0},{3,1},{6,4},{7,5},{10,8},{11,9},{14,12},{15,13},{18,16},{19,... | collective-permute-start | bytes 36872 | tf_op jit(solution)/shard_map/ppermute | solution.py:26
  169.6 5.9 %copy-start.10 = (s32[1,1,512]{2,1,0:T(1,128)S(1)}, s32[1,1,512]{2,1,0:T(1,128)}, u32[]{:S(2)}) copy-start(s32[1,1,512]{2,1,0:T(1,128)} %param.14) | copy-start | bytes 6148
  169.6 20.3 %collective-permute-start.4 = (f32[6,16,12,4]{1,3,2,0:T(4,128)S(1)}, f32[6,16,12,4]{1,3,2,0:T(4,128)S(1)}, u32[]{:S(2)}, u32[]{:S(2)}) collective-permute-start(f32[6,16,12,4]{1,3,2,0:T(4,128)S(1)} %get-tuple-element.204), channel_id=1, source_target_pairs={{0,1},{2,3},{4,5},{6,7},{8,9},{10,11},{12,13},{14,15},{16,17},{18,... | collective-permute-start | bytes 55304 | tf_op jit(solution)/shard_map/ppermute | solution.py:24
  170.9 19.5 %collective-permute-start.5 = (f32[6,16,12,4]{1,3,2,0:T(4,128)S(1)}, f32[6,16,12,4]{1,3,2,0:T(4,128)S(1)}, u32[]{:S(2)}, u32[]{:S(2)}) collective-permute-start(f32[6,16,12,4]{1,3,2,0:T(4,128)S(1)} %get-tuple-element.205), channel_id=1, source_target_pairs={{1,0},{3,2},{5,4},{7,6},{9,8},{11,10},{13,12},{15,14},{17,16},{19,... | collective-permute-start | bytes 55304 | tf_op jit(solution)/shard_map/ppermute | solution.py:26
  180.8 0.7 copy-start.11
  191.5 0.7 copy-start.5
  191.5 0.8 copy-start.6
  193.0 4.4 %collective-permute-start.6 = (f32[3,4,4,8]{3,2,1,0:T(4,128)S(1)}, f32[3,4,4,8]{3,2,1,0:T(4,128)S(1)}, u32[]{:S(2)}, u32[]{:S(2)}) collective-permute-start(f32[3,4,4,8]{3,2,1,0:T(4,128)S(1)} %get-tuple-element.221), channel_id=1, source_target_pairs={{4,0},{8,4},{12,8},{16,12},{20,16},{24,20},{28,24},{5,1},{9,5},{13... | collective-permute-start | bytes 4616 | tf_op jit(solution)/shard_map/ppermute | solution.py:26
  194.3 3.9 %collective-permute-start.7 = (f32[3,4,4,8]{3,2,1,0:T(4,128)S(1)}, f32[3,4,4,8]{3,2,1,0:T(4,128)S(1)}, u32[]{:S(2)}, u32[]{:S(2)}) collective-permute-start(f32[3,4,4,8]{3,2,1,0:T(4,128)S(1)} %get-tuple-element.220), channel_id=1, source_target_pairs={{0,4},{4,8},{8,12},{12,16},{16,20},{20,24},{24,28},{1,5},{5,9},{9,... | collective-permute-start | bytes 4616 | tf_op jit(solution)/shard_map/ppermute | solution.py:24
  198.2 3.5 %collective-permute-start.8 = (f32[3,16,4,8]{3,2,1,0:T(4,128)S(1)}, f32[3,16,4,8]{3,2,1,0:T(4,128)S(1)}, u32[]{:S(2)}, u32[]{:S(2)}) collective-permute-start(f32[3,16,4,8]{3,2,1,0:T(4,128)S(1)} %pad_maximum_fusion.14), channel_id=1, source_target_pairs={{2,0},{3,1},{6,4},{7,5},{10,8},{11,9},{14,12},{15,13},{18,16},{19,... | collective-permute-start | bytes 18440 | tf_op jit(solution)/shard_map/ppermute | solution.py:26
  199.5 6.5 %collective-permute-start.9 = (f32[3,16,4,8]{3,2,1,0:T(4,128)S(1)}, f32[3,16,4,8]{3,2,1,0:T(4,128)S(1)}, u32[]{:S(2)}, u32[]{:S(2)}) collective-permute-start(f32[3,16,4,8]{3,2,1,0:T(4,128)S(1)} %pad_maximum_fusion.14), channel_id=1, source_target_pairs={{0,2},{1,3},{4,6},{5,7},{8,10},{9,11},{12,14},{13,15},{16,18},{17,... | collective-permute-start | bytes 18440 | tf_op jit(solution)/shard_map/ppermute | solution.py:24
  206.2 18.2 %collective-permute-start.10 = (f32[3,16,12,4]{3,2,1,0:T(8,128)S(1)}, f32[3,16,12,4]{3,2,1,0:T(8,128)S(1)}, u32[]{:S(2)}, u32[]{:S(2)}) collective-permute-start(f32[3,16,12,4]{3,2,1,0:T(8,128)S(1)} %get-tuple-element.202), channel_id=1, source_target_pairs={{1,0},{3,2},{5,4},{7,6},{9,8},{11,10},{13,12},{15,14},{17,16},{19,... | collective-permute-start | bytes 27656 | tf_op jit(solution)/shard_map/ppermute | solution.py:26
  210.1 14.3 %collective-permute-start.11 = (f32[3,16,12,4]{3,2,1,0:T(8,128)S(1)}, f32[3,16,12,4]{3,2,1,0:T(8,128)S(1)}, u32[]{:S(2)}, u32[]{:S(2)}) collective-permute-start(f32[3,16,12,4]{3,2,1,0:T(8,128)S(1)} %get-tuple-element.203), channel_id=1, source_target_pairs={{0,1},{2,3},{4,5},{6,7},{8,9},{10,11},{12,13},{14,15},{16,17},{18,... | collective-permute-start | bytes 27656 | tf_op jit(solution)/shard_map/ppermute | solution.py:24
  213.5 16.1 %all-to-all-start = ((f32[16,1,336]{2,1,0:T(1,128)}), f32[16,1,336]{2,1,0:T(1,128)S(1)}, u32[]{:S(2)}, u32[]{:S(2)}) async-start(f32[16,1,336]{2,1,0:T(1,128)} %reshape.481), calls=%async_computation.1 | async-start | bytes 49152 | tf_op jit(solution)/shard_map/all_to_all | solution.py:206
  230.9 1.7 copy-start
  232.6 0.9 copy-start.2
  233.8 3.3 %collective-permute-start.12 = (f32[6,4,4,8]{3,2,1,0:T(4,128)S(1)}, f32[6,4,4,8]{3,2,1,0:T(4,128)S(1)}, u32[]{:S(2)}, u32[]{:S(2)}) collective-permute-start(f32[6,4,4,8]{3,2,1,0:T(4,128)S(1)} %get-tuple-element.212), channel_id=1, source_target_pairs={{0,4},{4,8},{8,12},{12,16},{16,20},{20,24},{24,28},{1,5},{5,9},{9,... | collective-permute-start | bytes 9224 | tf_op jit(solution)/shard_map/ppermute | solution.py:24
  235.8 3.2 %collective-permute-start.13 = (f32[6,4,4,8]{3,2,1,0:T(4,128)S(1)}, f32[6,4,4,8]{3,2,1,0:T(4,128)S(1)}, u32[]{:S(2)}, u32[]{:S(2)}) collective-permute-start(f32[6,4,4,8]{3,2,1,0:T(4,128)S(1)} %get-tuple-element.213), channel_id=1, source_target_pairs={{4,0},{8,4},{12,8},{16,12},{20,16},{24,20},{28,24},{5,1},{9,5},{13... | collective-permute-start | bytes 9224 | tf_op jit(solution)/shard_map/ppermute | solution.py:26
  239.1 7.9 %collective-permute-start.14 = (f32[6,16,4,8]{3,2,1,0:T(4,128)S(1)}, f32[6,16,4,8]{3,2,1,0:T(4,128)S(1)}, u32[]{:S(2)}, u32[]{:S(2)}) collective-permute-start(f32[6,16,4,8]{3,2,1,0:T(4,128)S(1)} %pad_maximum_fusion.12), channel_id=1, source_target_pairs={{0,2},{1,3},{4,6},{5,7},{8,10},{9,11},{12,14},{13,15},{16,18},{17,... | collective-permute-start | bytes 36872 | tf_op jit(solution)/shard_map/ppermute | solution.py:24
  240.4 8.3 %collective-permute-start.15 = (f32[6,16,4,8]{3,2,1,0:T(4,128)S(1)}, f32[6,16,4,8]{3,2,1,0:T(4,128)S(1)}, u32[]{:S(2)}, u32[]{:S(2)}) collective-permute-start(f32[6,16,4,8]{3,2,1,0:T(4,128)S(1)} %pad_maximum_fusion.12), channel_id=1, source_target_pairs={{2,0},{3,1},{6,4},{7,5},{10,8},{11,9},{14,12},{15,13},{18,16},{19,... | collective-permute-start | bytes 36872 | tf_op jit(solution)/shard_map/ppermute | solution.py:26
  249.7 7.7 %collective-permute-start.16 = (f32[6,16,12,4]{1,3,2,0:T(4,128)S(1)}, f32[6,16,12,4]{1,3,2,0:T(4,128)S(1)}, u32[]{:S(2)}, u32[]{:S(2)}) collective-permute-start(f32[6,16,12,4]{1,3,2,0:T(4,128)S(1)} %copy.90), channel_id=1, source_target_pairs={{0,1},{2,3},{4,5},{6,7},{8,9},{10,11},{12,13},{14,15},{16,17},{18,... | collective-permute-start | bytes 55304 | tf_op jit(solution)/shard_map/ppermute | solution.py:24
  251.5 8.1 %collective-permute-start.17 = (f32[6,16,12,4]{1,3,2,0:T(4,128)S(1)}, f32[6,16,12,4]{1,3,2,0:T(4,128)S(1)}, u32[]{:S(2)}, u32[]{:S(2)}) collective-permute-start(f32[6,16,12,4]{1,3,2,0:T(4,128)S(1)} %copy.91), channel_id=1, source_target_pairs={{1,0},{3,2},{5,4},{7,6},{9,8},{11,10},{13,12},{15,14},{17,16},{19,... | collective-permute-start | bytes 55304 | tf_op jit(solution)/shard_map/ppermute | solution.py:26
  261.7 34.7 %copy-start.1 = (f32[3,8,4,8]{3,2,1,0:T(4,128)}, f32[3,8,4,8]{3,2,1,0:T(4,128)S(1)}, u32[]{:S(2)}) copy-start(f32[3,8,4,8]{3,2,1,0:T(4,128)S(1)} %divide_add_fusion) | copy-start | bytes 9220
  261.7 4.6 %collective-permute-start.18 = (f32[3,4,4,8]{3,2,1,0:T(4,128)S(1)}, f32[3,4,4,8]{3,2,1,0:T(4,128)S(1)}, u32[]{:S(2)}, u32[]{:S(2)}) collective-permute-start(f32[3,4,4,8]{3,2,1,0:T(4,128)S(1)} %get-tuple-element.219), channel_id=1, source_target_pairs={{4,0},{8,4},{12,8},{16,12},{20,16},{24,20},{28,24},{5,1},{9,5},{13... | collective-permute-start | bytes 4616 | tf_op jit(solution)/shard_map/ppermute | solution.py:26
  263.0 4.2 %collective-permute-start.19 = (f32[3,4,4,8]{3,2,1,0:T(4,128)S(1)}, f32[3,4,4,8]{3,2,1,0:T(4,128)S(1)}, u32[]{:S(2)}, u32[]{:S(2)}) collective-permute-start(f32[3,4,4,8]{3,2,1,0:T(4,128)S(1)} %get-tuple-element.218), channel_id=1, source_target_pairs={{0,4},{4,8},{8,12},{12,16},{16,20},{20,24},{24,28},{1,5},{5,9},{9,... | collective-permute-start | bytes 4616 | tf_op jit(solution)/shard_map/ppermute | solution.py:24
  267.2 6.6 %collective-permute-start.20 = (f32[3,16,4,8]{3,2,1,0:T(4,128)S(1)}, f32[3,16,4,8]{3,2,1,0:T(4,128)S(1)}, u32[]{:S(2)}, u32[]{:S(2)}) collective-permute-start(f32[3,16,4,8]{3,2,1,0:T(4,128)S(1)} %pad_maximum_fusion.15), channel_id=1, source_target_pairs={{2,0},{3,1},{6,4},{7,5},{10,8},{11,9},{14,12},{15,13},{18,16},{19,... | collective-permute-start | bytes 18440 | tf_op jit(solution)/shard_map/ppermute | solution.py:26
  271.6 6.5 %collective-permute-start.21 = (f32[3,16,4,8]{3,2,1,0:T(4,128)S(1)}, f32[3,16,4,8]{3,2,1,0:T(4,128)S(1)}, u32[]{:S(2)}, u32[]{:S(2)}) collective-permute-start(f32[3,16,4,8]{3,2,1,0:T(4,128)S(1)} %pad_maximum_fusion.15), channel_id=1, source_target_pairs={{0,2},{1,3},{4,6},{5,7},{8,10},{9,11},{12,14},{13,15},{16,18},{17,... | collective-permute-start | bytes 18440 | tf_op jit(solution)/shard_map/ppermute | solution.py:24
  278.4 13.9 %collective-permute-start.22 = (f32[3,16,12,4]{3,2,1,0:T(8,128)S(1)}, f32[3,16,12,4]{3,2,1,0:T(8,128)S(1)}, u32[]{:S(2)}, u32[]{:S(2)}) collective-permute-start(f32[3,16,12,4]{3,2,1,0:T(8,128)S(1)} %get-tuple-element.200), channel_id=1, source_target_pairs={{1,0},{3,2},{5,4},{7,6},{9,8},{11,10},{13,12},{15,14},{17,16},{19,... | collective-permute-start | bytes 27656 | tf_op jit(solution)/shard_map/ppermute | solution.py:26
  282.8 13.6 %collective-permute-start.23 = (f32[3,16,12,4]{3,2,1,0:T(8,128)S(1)}, f32[3,16,12,4]{3,2,1,0:T(8,128)S(1)}, u32[]{:S(2)}, u32[]{:S(2)}) collective-permute-start(f32[3,16,12,4]{3,2,1,0:T(8,128)S(1)} %get-tuple-element.201), channel_id=1, source_target_pairs={{0,1},{2,3},{4,5},{6,7},{8,9},{10,11},{12,13},{14,15},{16,17},{18,... | collective-permute-start | bytes 27656 | tf_op jit(solution)/shard_map/ppermute | solution.py:24
  297.5 0.6 copy-start.9
Sparse Core Ops, SparseCore 0:
  178.3 14.7 reduce-scatter.1
where the time goes:
time: 308 us; the launch traced here: 305 us
  other arithmetic  134 us (44%)
  starting transfers between devices  68.9 us (22%)
  local copies, waits for them, and re-layouts  43 us (14%)
  waiting for transfers between devices  37 us (12%)
  between operations  15.5 us (5%)
  blocking collectives  6.73 us (2%)
    add x15, other arithmetic, ordered_sum(): running = running + summand  122 us
    ppermute x12, starting transfers between devices, with_halo(): lax.ppermute(head, axis, [((i + 1) % count, i) for i in range(ends)])  37.4 us
    gather x4, local copies, waits for them, and re-layouts, absorb(): picked = jnp.take(table, chosen, axis=1)  21.9 us
    ppermute x12, starting transfers between devices, with_halo(): lax.ppermute(tail, axis, [(i, (i + 1) % count) for i in range(ends)])  20.5 us
    ppermute x12, waiting for transfers between devices, with_halo(): lax.ppermute(tail, axis, [(i, (i + 1) % count) for i in range(ends)])  17.7 us
    ppermute x12, waiting for transfers between devices, with_halo(): lax.ppermute(head, axis, [((i + 1) % count, i) for i in range(ends)])  15.1 us
    all_to_all x1, starting transfers between devices, on_device(): lax.all_to_all(averaged, ('gx', 'gy'), split_axis=1, concat_axis=1, tiled...  11 us
    unnamed x29, local copies, waits for them, and re-layouts  7.27 us
  transfers between devices with their start and end apart: 26, of which 14 were waited for; matrix products, arithmetic and copies ran while one was open for 53% of the time, Pallas kernels for 0%

commit v1 on v0

--- a/solution.py
+++ b/solution.py
@@ -11,6 +11,23 @@
 upper_pairs = [
     (row_index, col_index) for row_index in range(6) for col_index in range(row_index, 6)
 ]
+
+
+def spread_streams_here(slab_in, array_dim, x_in):
+    r1 = slab_in.shape
+    front = jnp.moveaxis(
+        slab_in.reshape(*r1[:array_dim], x_in, r1[array_dim] // x_in, *r1[array_dim + 1 :]),
+        array_dim,
+        0,
+    )
+    return front
+
+
+def halves_update(u_in, dim_no):
+    near = list(u_in.shape[1:])
+    near[dim_no] *= u_in.shape[0]
+    a_next = jnp.moveaxis(u_in, 0, dim_no).reshape(near)
+    return a_next
 
 
 def with_halo(cells, sides, width):
@@ -203,7 +220,25 @@
         lax.psum_scatter(counted, "ga", scatter_dimension=3, tiled=True),
     )
     averaged = placed / counted[None]
-    moved = lax.all_to_all(averaged, ("gx", "gy"), split_axis=1, concat_axis=1, tiled=True)
+
+    def begin_grid_for(state, my_tile, comm_axis, array_here):
+        local_part, local_next = (lax.axis_size(comm_axis), lax.axis_index(comm_axis))
+        q_next = spread_streams_here(my_tile, state, local_part)
+        seen = [q_next[local_next]]
+        k = 1
+        while k < local_part:
+            o_now = q_next[(local_next + k) % local_part]
+            seen.append(
+                lax.ppermute(
+                    o_now, comm_axis, [(h, (h + k) % local_part) for h in range(local_part)]
+                )
+            )
+            k += 1
+        q_next = jnp.stack(seen)[(local_next - jnp.arange(local_part)) % local_part]
+        r_now = halves_update(q_next, array_here)
+        return r_now
+
+    moved = begin_grid_for(1, averaged, ("gx", "gy"), 1)
     moved = moved.reshape(21, part_x, part_y, sub_x, sub_y, brick_z)
     stiffness = moved.transpose(0, 1, 3, 2, 4, 5).reshape(21, brick_x, brick_y, brick_z)
     for step_index in range(STEPS):

time: 308 us -> 334 us (1.084)
  starting transfers between devices: 68.9 us -> 84 us
  waiting for transfers between devices: 37 us -> 49.4 us
    ppermute x0 -> x15, starting transfers between devices: none -> 23 us  [begin_grid_for(): lax.ppermute(o_now, comm_axis, [(h, (h + k) % local_part) for h in range(...]
    all_to_all x1 -> x0, starting transfers between devices: 11 us -> none  [on_device(): lax.all_to_all(averaged, ('gx', 'gy'), split_axis=1, concat_axis=1, tiled...]
    ppermute x12, waiting for transfers between devices: 15.1 us -> 23.5 us  [with_halo(): lax.ppermute(head, axis, [((i + 1) % count, i) for i in range(ends)])]
    ppermute x12, waiting for transfers between devices: 17.7 us -> 24.5 us  [with_halo(): lax.ppermute(tail, axis, [(i, (i + 1) % count) for i in range(ends)])]
    all_to_all x1 -> x0, waiting for transfers between devices: 4.25 us -> none  [on_device(): lax.all_to_all(averaged, ('gx', 'gy'), split_axis=1, concat_axis=1, tiled...]
    ppermute x12, starting transfers between devices: 37.4 us -> 41.5 us  [with_halo(): lax.ppermute(head, axis, [((i + 1) % count, i) for i in range(ends)])]
    unnamed x29 -> x42, local copies, waits for them, and re-layouts: 7.27 us -> 6.44 us
  transfers between devices with their start and end apart: 26 -> 40, of which waited for: 14 -> 20; matrix products, arithmetic and copies ran while one was open for 53% -> 49% of each run, Pallas kernels for 0% -> 0%
where the time goes in v1:
time: 334 us; the launch traced here: 332 us
  other arithmetic  133 us (40%)
  starting transfers between devices  84 us (25%)
  waiting for transfers between devices  49.4 us (15%)
  local copies, waits for them, and re-layouts  42 us (13%)
  between operations  15.7 us (5%)
  blocking collectives  7.16 us (2%)
    add x15, other arithmetic, ordered_sum(): running = running + summand  122 us
    ppermute x12, starting transfers between devices, with_halo(): lax.ppermute(head, axis, [((i + 1) % count, i) for i in range(ends)])  41.5 us
    ppermute x12, waiting for transfers between devices, with_halo(): lax.ppermute(tail, axis, [(i, (i + 1) % count) for i in range(ends)])  24.5 us
    ppermute x12, waiting for transfers between devices, with_halo(): lax.ppermute(head, axis, [((i + 1) % count, i) for i in range(ends)])  23.5 us
    ppermute x15, starting transfers between devices, begin_grid_for(): lax.ppermute(o_now, comm_axis, [(h, (h + k) % local_part) for h in range(...  23 us
    gather x4, local copies, waits for them, and re-layouts, absorb(): picked = jnp.take(table, chosen, axis=1)  21.9 us
    ppermute x12, starting transfers between devices, with_halo(): lax.ppermute(tail, axis, [(i, (i + 1) % count) for i in range(ends)])  19.5 us
    unnamed x1, blocking collectives  7.16 us
  transfers between devices with their start and end apart: 40, of which 20 were waited for; matrix products, arithmetic and copies ran while one was open for 49% of the time, Pallas kernels for 0%

profile of v1, /device:TPU:6, one launch (start us, length us, event | category | flops | bytes accessed | tf_op | source)
XLA Modules:
  0.0 331.6 jit_solution(9157314191996244677)
XLA Ops:
  8.3 1.7 collective-permute-start.15
  10.0 1.3 collective-permute-start.16
  13.4 14.1 %multiply_add_fusion.6 = (f32[1,2048]{1,0:T(1,128)S(1)}, f32[1,2048]{1,0:T(1,128)S(1)}, f32[1,2048]{1,0:T(1,128)S(1)}, f32[1,2048]{1,0:T(1,128)S(1)}, f32[1,2048...) fusion(f32[]{:T(128)} %bitcast.22, f32[]{:T(128)} %bitcast.21, ...), kind=kLoop, calls=%fused_computation.312 | loop fusion | flops 219136 | bytes 131156 | tf_op jit(solution)/shard_map/add | solution.py:57
  27.5 13.8 %multiply_add_fusion.7 = (f32[1,2048]{1,0:T(1,128)S(1)}, f32[1,2048]{1,0:T(1,128)S(1)}, f32[1,2048]{1,0:T(1,128)S(1)}, f32[1,2048]{1,0:T(1,128)S(1)}, f32[1,2048...) fusion(f32[1,2048]{1,0:T(1,128)S(1)} %get-tuple-element.135, ...), kind=kLoop, calls=%fused_computation.313 | loop fusion | flops 186368 | bytes 163924 | tf_op jit(solution)/shard_map/add | solution.py:57
  41.3 13.6 %multiply_add_fusion.15 = (f32[1,2048]{1,0:T(1,128)S(1)}, f32[1,2048]{1,0:T(1,128)S(1)}, f32[1,2048]{1,0:T(1,128)S(1)}, f32[1,2048]{1,0:T(1,128)S(1)}, f32[1,204...) fusion(f32[1,2048]{1,0:T(1,128)S(1)} %get-tuple-element.135, f32[1,2048]{1,0:T(1,128)S(1)} %get-tuple-element.134, ...), kind=kLoop, calls=%fused_computation.321 | loop fusion | flops 182272 | bytes 155732 | tf_op jit(solution)/shard_map/add | solution.py:57
  54.9 13.3 %multiply_add_fusion.8 = f32[1,2048]{1,0:T(1,128)S(1)} fusion(f32[1,2048]{1,0:T(1,128)S(1)} %get-tuple-element.148, f32[1,2048]{1,0:T(1,128)S(1)} %get-tuple-element.147, f32[1,2048]{1,0:T(1,128)S(1)} %get-tuple-element.146, f32[1,2048]{1,0:T(1,128)S(1)} %get-tuple-element.145, f32[1,2048]{1,0:T(1,128)S(1)} %get-tuple-element.144, ...), kind=kLoop, calls=%fused_computation.314 | loop fusion | flops 157696 | bytes 57428 | tf_op jit(solution)/shard_map/add | solution.py:57
  68.2 13.3 %multiply_add_fusion.16 = f32[1,2048]{1,0:T(1,128)S(1)} fusion(f32[1,2048]{1,0:T(1,128)S(1)} %get-tuple-element.148, f32[1,2048]{1,0:T(1,128)S(1)} %get-tuple-element.147, f32[1,2048]{1,0:T(1,128)S(1)} %get-tuple-element.146, f32[1,2048]{1,0:T(1,128)S(1)} %get-tuple-element.145, f32[1,2048]{1,0:T(1,128)S(1)} %get-tuple-element.144, ...), kind=kLoop, calls=%fused_computation.322 | loop fusion | flops 157696 | bytes 106580 | tf_op jit(solution)/shard_map/add | solution.py:57
  81.5 13.3 %multiply_add_fusion.17 = f32[1,2048]{1,0:T(1,128)S(1)} fusion(f32[1,2048]{1,0:T(1,128)S(1)} %get-tuple-element.157, f32[1,2048]{1,0:T(1,128)S(1)} %get-tuple-element.156, f32[1,2048]{1,0:T(1,128)S(1)} %get-tuple-element.155, f32[1,2048]{1,0:T(1,128)S(1)} %get-tuple-element.154, f32[1,2048]{1,0:T(1,128)S(1)} %get-tuple-element.153, ...), kind=kLoop, calls=%fused_computation.323 | loop fusion | flops 157696 | bytes 57428 | tf_op jit(solution)/shard_map/add | solution.py:57
  94.8 13.3 %multiply_add_fusion.34 = (f32[1,2048]{1,0:T(1,128)S(1)}, f32[1,2048]{1,0:T(1,128)S(1)}, f32[1,2048]{1,0:T(1,128)S(1)}, f32[1,2048]{1,0:T(1,128)S(1)}, f32[1,204...) fusion(f32[1,2048]{1,0:T(1,128)S(1)} %get-tuple-element.135, ...), kind=kLoop, calls=%fused_computation.340 | loop fusion | flops 174080 | bytes 155732 | tf_op jit(solution)/shard_map/add | solution.py:57
  108.1 13.5 %multiply_add_fusion.24 = (f32[1,2048]{1,0:T(1,128)S(1)}, f32[1,2048]{1,0:T(1,128)S(1)}, f32[1,2048]{1,0:T(1,128)S(1)}, f32[1,2048]{1,0:T(1,128)S(1)}, f32[1,204...) fusion(f32[1,2048]{1,0:T(1,128)S(1)} %get-tuple-element.135, ...), kind=kLoop, calls=%fused_computation.330 | loop fusion | flops 174080 | bytes 139348 | tf_op jit(solution)/shard_map/add | solution.py:57
  121.8 13.3 %multiply_add_fusion.45 = (f32[1,2048]{1,0:T(1,128)S(1)}, f32[1,2048]{1,0:T(1,128)S(1)}, f32[1,2048]{1,0:T(1,128)S(1)}, f32[1,2048]{1,0:T(1,128)S(1)}, f32[1,204...) fusion(f32[1,2048]{1,0:T(1,128)S(1)} %get-tuple-element.135, ...), kind=kLoop, calls=%fused_computation.351 | loop fusion | flops 174080 | bytes 155732 | tf_op jit(solution)/shard_map/add | solution.py:57
  137.8 25.7 %while.13 = (s32[]{:T(128)}, f32[21,512]{0,1:T(8,128)S(1)}, f32[512]{0:T(512)S(1)}, s32[4,4,512]{2,1,0:T(4,128)S(1)}, f32[21,2048]{0,1:T(8,128)S(1)}, /*index=5*/bf16[4,4,512]{2,1,0:T(4,128)(2,1)S(1)}, s32[]{:T(128)}, s32[]{:T(128)}) while((s32[]{:T(128)}, f32[21,512]{0,1:T(8,128)S(1)}, f32[512]{0:T(512)S(1)}, ...), condition=%wide.region_3.4_spmd.clone, body=%wide.region_0.3_spmd.clone.sunk | while | flops 166915 | bytes 790640 | solution.py:128
  137.8 5.5 %gather_fusion = f32[2048,21]{1,0:T(8,128)S(1)} fusion(f32[21,2048]{0,1:T(8,128)S(1)} %get-tuple-element.325, s32[2048]{0:T(1024)S(1)} %broadcast_clamp_fusion.2), kind=kCustom, calls=%fused_computation.clone.clone.1 | custom fusion | bytes 352256 | tf_op jit(solution)/shard_map/while/body/eval_jaxpr/jit(_take)/gather | solution.py:117
  144.2 5.5 %gather_fusion = f32[2048,21]{1,0:T(8,128)S(1)} fusion(f32[21,2048]{0,1:T(8,128)S(1)} %get-tuple-element.325, s32[2048]{0:T(1024)S(1)} %broadcast_clamp_fusion.2), kind=kCustom, calls=%fused_computation.clone.clone.1 | custom fusion | bytes 352256 | tf_op jit(solution)/shard_map/while/body/eval_jaxpr/jit(_take)/gather | solution.py:117
  150.7 5.5 %gather_fusion = f32[2048,21]{1,0:T(8,128)S(1)} fusion(f32[21,2048]{0,1:T(8,128)S(1)} %get-tuple-element.325, s32[2048]{0:T(1024)S(1)} %broadcast_clamp_fusion.2), kind=kCustom, calls=%fused_computation.clone.clone.1 | custom fusion | bytes 352256 | tf_op jit(solution)/shard_map/while/body/eval_jaxpr/jit(_take)/gather | solution.py:117
  157.1 5.5 %gather_fusion = f32[2048,21]{1,0:T(8,128)S(1)} fusion(f32[21,2048]{0,1:T(8,128)S(1)} %get-tuple-element.325, s32[2048]{0:T(1024)S(1)} %broadcast_clamp_fusion.2), kind=kCustom, calls=%fused_computation.clone.clone.1 | custom fusion | bytes 352256 | tf_op jit(solution)/shard_map/while/body/eval_jaxpr/jit(_take)/gather | solution.py:117
  163.5 2.4 scatter_custom_fusion
  166.0 2.4 scatter_custom_fusion.1
  168.6 7.2 %all-reduce = f32[16,1,2,16]{0,2,1,3:T(2,128)S(1)} all-reduce(f32[16,1,2,16]{0,2,1,3:T(2,128)S(1)} %copy.156), channel_id=3, replica_groups=mesh['gx'=8,'gy'=2,'ga'=2] {'ga'}, use_global_device_ids=true, to_apply=%region_7.8.clone | all-reduce | flops 512 | bytes 4096
  177.8 1.3 collective-permute-start.17
  179.1 4.6 %collective-permute-start.18 = (f32[6,16,4,8]{1,3,2,0:T(8,128)S(1)}, f32[6,16,4,8]{1,3,2,0:T(8,128)S(1)}, u32[]{:S(2)}, u32[]{:S(2)}) collective-permute-start(f32[6,16,4,8]{1,3,2,0:T(8,128)S(1)} %pad_maximum_fusion.13), channel_id=1, source_target_pairs={{2,0},{3,1},{6,4},{7,5},{10,8},{11,9},{14,12},{15,13},{18,16},{19,... | collective-permute-start | bytes 36872 | tf_op jit(solution)/shard_map/ppermute | solution.py:43
  186.2 1.3 collective-permute-start.19
  187.5 4.7 %collective-permute-start.20 = (f32[6,16,12,4]{1,3,2,0:T(4,128)S(1)}, f32[6,16,12,4]{1,3,2,0:T(4,128)S(1)}, u32[]{:S(2)}, u32[]{:S(2)}) collective-permute-start(f32[6,16,12,4]{1,3,2,0:T(4,128)S(1)} %get-tuple-element.205), channel_id=1, source_target_pairs={{1,0},{3,2},{5,4},{7,6},{9,8},{11,10},{13,12},{15,14},{17,16},{19,... | collective-permute-start | bytes 55304 | tf_op jit(solution)/shard_map/ppermute | solution.py:43
  197.3 1.3 collective-permute-start.21
  198.6 3.0 collective-permute-start.22
  202.5 4.4 %collective-permute-start.23 = (f32[3,16,4,8]{3,2,1,0:T(4,128)S(1)}, f32[3,16,4,8]{3,2,1,0:T(4,128)S(1)}, u32[]{:S(2)}, u32[]{:S(2)}) collective-permute-start(f32[3,16,4,8]{3,2,1,0:T(4,128)S(1)} %pad_maximum_fusion.14), channel_id=1, source_target_pairs={{2,0},{3,1},{6,4},{7,5},{10,8},{11,9},{14,12},{15,13},{18,16},{19,... | collective-permute-start | bytes 18440 | tf_op jit(solution)/shard_map/ppermute | solution.py:43
  206.9 1.3 collective-permute-start.24
  209.1 4.3 %collective-permute-done.24 = f32[3,16,4,8]{3,2,1,0:T(4,128)S(1)} collective-permute-done((f32[3,16,4,8]{3,2,1,0:T(4,128)S(1)}, f32[3,16,4,8]{3,2,1,0:T(4,128)S(1)}, u32[]{:S(2)}, u32[]{:S(2)}) %collective-permute-start.24) | collective-permute-done | bytes 6176 | tf_op jit(solution)/shard_map/ppermute | solution.py:41
  213.7 4.4 %collective-permute-start.25 = (f32[3,16,12,4]{3,2,1,0:T(8,128)S(1)}, f32[3,16,12,4]{3,2,1,0:T(8,128)S(1)}, u32[]{:S(2)}, u32[]{:S(2)}) collective-permute-start(f32[3,16,12,4]{3,2,1,0:T(8,128)S(1)} %get-tuple-element.202), channel_id=1, source_target_pairs={{1,0},{3,2},{5,4},{7,6},{9,8},{11,10},{13,12},{15,14},{17,16},{19,... | collective-permute-start | bytes 27656 | tf_op jit(solution)/shard_map/ppermute | solution.py:43
  218.1 1.3 collective-permute-start.26
  219.5 6.7 %collective-permute-done.25 = f32[3,16,12,4]{3,2,1,0:T(8,128)S(1)} collective-permute-done((f32[3,16,12,4]{3,2,1,0:T(8,128)S(1)}, f32[3,16,12,4]{3,2,1,0:T(8,128)S(1)}, u32[]{:S(2)}, u32[]{:S(2)}) %collective-permute-start.25) | collective-permute-done | bytes 9248 | tf_op jit(solution)/shard_map/ppermute | solution.py:43
  226.2 4.7 %collective-permute-done.26 = f32[3,16,12,4]{3,2,1,0:T(8,128)S(1)} collective-permute-done((f32[3,16,12,4]{3,2,1,0:T(8,128)S(1)}, f32[3,16,12,4]{3,2,1,0:T(8,128)S(1)}, u32[]{:S(2)}, u32[]{:S(2)}) %collective-permute-start.26) | collective-permute-done | bytes 9248 | tf_op jit(solution)/shard_map/ppermute | solution.py:41
  233.1 3.1 collective-permute-start.1
  236.1 2.0 collective-permute-start.2
  238.1 1.6 collective-permute-start.3
  239.8 2.2 collective-permute-start.5
  242.0 2.5 collective-permute-start.6
  244.6 1.2 collective-permute-start.7
  246.6 2.1 collective-permute-start.9
  248.7 2.1 collective-permute-start.10
  252.2 1.5 collective-permute-start.13
  253.7 2.3 collective-permute-start.14
  256.1 1.3 collective-permute-done.14
  257.9 1.7 slice_reduce_fusion
  260.8 1.3 collective-permute-start.27
  262.1 1.3 collective-permute-start.28
  263.4 2.1 collective-permute-done.28
  265.5 1.3 collective-permute-start.29
  266.8 4.6 %collective-permute-start.30 = (f32[6,16,4,8]{3,2,1,0:T(4,128)S(1)}, f32[6,16,4,8]{3,2,1,0:T(4,128)S(1)}, u32[]{:S(2)}, u32[]{:S(2)}) collective-permute-start(f32[6,16,4,8]{3,2,1,0:T(4,128)S(1)} %pad_maximum_fusion.12), channel_id=1, source_target_pairs={{2,0},{3,1},{6,4},{7,5},{10,8},{11,9},{14,12},{15,13},{18,16},{19,... | collective-permute-start | bytes 36872 | tf_op jit(solution)/shard_map/ppermute | solution.py:43
  271.4 2.0 collective-permute-done.29
  273.4 1.7 collective-permute-done.30
  276.1 1.3 collective-permute-start.31
  277.9 4.5 %collective-permute-start.32 = (f32[6,16,12,4]{1,3,2,0:T(4,128)S(1)}, f32[6,16,12,4]{1,3,2,0:T(4,128)S(1)}, u32[]{:S(2)}, u32[]{:S(2)}) collective-permute-start(f32[6,16,12,4]{1,3,2,0:T(4,128)S(1)} %copy.179), channel_id=1, source_target_pairs={{1,0},{3,2},{5,4},{7,6},{9,8},{11,10},{13,12},{15,14},{17,16},{19,... | collective-permute-start | bytes 55304 | tf_op jit(solution)/shard_map/ppermute | solution.py:43
  282.5 1.5 collective-permute-done.31
  284.6 1.7 collective-permute-done.32
  288.4 1.3 collective-permute-start.33
  289.7 3.1 collective-permute-start.34
  293.6 4.7 %collective-permute-start.35 = (f32[3,16,4,8]{3,2,1,0:T(4,128)S(1)}, f32[3,16,4,8]{3,2,1,0:T(4,128)S(1)}, u32[]{:S(2)}, u32[]{:S(2)}) collective-permute-start(f32[3,16,4,8]{3,2,1,0:T(4,128)S(1)} %pad_maximum_fusion.15), channel_id=1, source_target_pairs={{2,0},{3,1},{6,4},{7,5},{10,8},{11,9},{14,12},{15,13},{18,16},{19,... | collective-permute-start | bytes 18440 | tf_op jit(solution)/shard_map/ppermute | solution.py:43
  298.3 1.3 collective-permute-start.36
  300.5 4.7 %collective-permute-done.36 = f32[3,16,4,8]{3,2,1,0:T(4,128)S(1)} collective-permute-done((f32[3,16,4,8]{3,2,1,0:T(4,128)S(1)}, f32[3,16,4,8]{3,2,1,0:T(4,128)S(1)}, u32[]{:S(2)}, u32[]{:S(2)}) %collective-permute-start.36) | collective-permute-done | bytes 6176 | tf_op jit(solution)/shard_map/ppermute | solution.py:41
  305.5 4.4 %collective-permute-start.37 = (f32[3,16,12,4]{3,2,1,0:T(8,128)S(1)}, f32[3,16,12,4]{3,2,1,0:T(8,128)S(1)}, u32[]{:S(2)}, u32[]{:S(2)}) collective-permute-start(f32[3,16,12,4]{3,2,1,0:T(8,128)S(1)} %get-tuple-element.200), channel_id=1, source_target_pairs={{1,0},{3,2},{5,4},{7,6},{9,8},{11,10},{13,12},{15,14},{17,16},{19,... | collective-permute-start | bytes 27656 | tf_op jit(solution)/shard_map/ppermute | solution.py:43
  309.9 1.3 collective-permute-start.38
  311.4 7.4 %collective-permute-done.37 = f32[3,16,12,4]{3,2,1,0:T(8,128)S(1)} collective-permute-done((f32[3,16,12,4]{3,2,1,0:T(8,128)S(1)}, f32[3,16,12,4]{3,2,1,0:T(8,128)S(1)}, u32[]{:S(2)}, u32[]{:S(2)}) %collective-permute-start.37) | collective-permute-done | bytes 9248 | tf_op jit(solution)/shard_map/ppermute | solution.py:43
  318.8 4.1 %collective-permute-done.38 = f32[3,16,12,4]{3,2,1,0:T(8,128)S(1)} collective-permute-done((f32[3,16,12,4]{3,2,1,0:T(8,128)S(1)}, f32[3,16,12,4]{3,2,1,0:T(8,128)S(1)}, u32[]{:S(2)}, u32[]{:S(2)}) %collective-permute-start.38) | collective-permute-done | bytes 9248 | tf_op jit(solution)/shard_map/ppermute | solution.py:41
  (188 shorter events, 34.7 us)
Async XLA Ops:
  7.2 224.6 %reduce-scatter.2.cloned.1.call-start = ((), (), s32[]{:S(2)}) async-start(), calls=%async_computation.1 | async-start | bytes 393216 | tf_op jit(solution)/shard_map/reduce_scatter | solution.py:219
  8.3 3.1 copy-start.3
  8.3 169.4 %collective-permute-start.15 = (f32[6,4,4,8]{1,3,2,0:T(8,128)S(1)}, f32[6,4,4,8]{1,3,2,0:T(8,128)S(1)}, u32[]{:S(2)}, u32[]{:S(2)}) collective-permute-start(f32[6,4,4,8]{1,3,2,0:T(8,128)S(1)} %get-tuple-element.229), channel_id=1, source_target_pairs={{0,4},{4,8},{8,12},{12,16},{16,20},{20,24},{24,28},{1,5},{5,9},{9,... | collective-permute-start | bytes 9224 | tf_op jit(solution)/shard_map/ppermute | solution.py:41
  10.0 167.6 %collective-permute-start.16 = (f32[6,4,4,8]{1,3,2,0:T(8,128)S(1)}, f32[6,4,4,8]{1,3,2,0:T(8,128)S(1)}, u32[]{:S(2)}, u32[]{:S(2)}) collective-permute-start(f32[6,4,4,8]{1,3,2,0:T(8,128)S(1)} %get-tuple-element.230), channel_id=1, source_target_pairs={{4,0},{8,4},{12,8},{16,12},{20,16},{24,20},{28,24},{5,1},{9,5},{13... | collective-permute-start | bytes 9224 | tf_op jit(solution)/shard_map/ppermute | solution.py:43
  12.7 0.8 copy-start.4
  136.2 0.8 copy-start.7
  137.0 0.7 copy-start.8
  137.8 25.7 %copy-start.10 = (s32[1,1,512]{2,1,0:T(1,128)S(1)}, s32[1,1,512]{2,1,0:T(1,128)}, u32[]{:S(2)}) copy-start(s32[1,1,512]{2,1,0:T(1,128)} %param.14) | copy-start | bytes 6148
  175.7 0.7 copy-start.11
  177.8 7.1 %collective-permute-start.17 = (f32[6,16,4,8]{1,3,2,0:T(8,128)S(1)}, f32[6,16,4,8]{1,3,2,0:T(8,128)S(1)}, u32[]{:S(2)}, u32[]{:S(2)}) collective-permute-start(f32[6,16,4,8]{1,3,2,0:T(8,128)S(1)} %pad_maximum_fusion.13), channel_id=1, source_target_pairs={{0,2},{1,3},{4,6},{5,7},{8,10},{9,11},{12,14},{13,15},{16,18},{17,... | collective-permute-start | bytes 36872 | tf_op jit(solution)/shard_map/ppermute | solution.py:41
  179.1 6.9 %collective-permute-start.18 = (f32[6,16,4,8]{1,3,2,0:T(8,128)S(1)}, f32[6,16,4,8]{1,3,2,0:T(8,128)S(1)}, u32[]{:S(2)}, u32[]{:S(2)}) collective-permute-start(f32[6,16,4,8]{1,3,2,0:T(8,128)S(1)} %pad_maximum_fusion.13), channel_id=1, source_target_pairs={{2,0},{3,1},{6,4},{7,5},{10,8},{11,9},{14,12},{15,13},{18,16},{19,... | collective-permute-start | bytes 36872 | tf_op jit(solution)/shard_map/ppermute | solution.py:43
  186.2 7.0 %collective-permute-start.19 = (f32[6,16,12,4]{1,3,2,0:T(4,128)S(1)}, f32[6,16,12,4]{1,3,2,0:T(4,128)S(1)}, u32[]{:S(2)}, u32[]{:S(2)}) collective-permute-start(f32[6,16,12,4]{1,3,2,0:T(4,128)S(1)} %get-tuple-element.204), channel_id=1, source_target_pairs={{0,1},{2,3},{4,5},{6,7},{8,9},{10,11},{12,13},{14,15},{16,17},{18,... | collective-permute-start | bytes 55304 | tf_op jit(solution)/shard_map/ppermute | solution.py:41
  187.5 7.2 %collective-permute-start.20 = (f32[6,16,12,4]{1,3,2,0:T(4,128)S(1)}, f32[6,16,12,4]{1,3,2,0:T(4,128)S(1)}, u32[]{:S(2)}, u32[]{:S(2)}) collective-permute-start(f32[6,16,12,4]{1,3,2,0:T(4,128)S(1)} %get-tuple-element.205), channel_id=1, source_target_pairs={{1,0},{3,2},{5,4},{7,6},{9,8},{11,10},{13,12},{15,14},{17,16},{19,... | collective-permute-start | bytes 55304 | tf_op jit(solution)/shard_map/ppermute | solution.py:43
  195.8 0.7 copy-start.5
  195.8 0.8 copy-start.6
  197.3 4.5 %collective-permute-start.21 = (f32[3,4,4,8]{3,2,1,0:T(4,128)S(1)}, f32[3,4,4,8]{3,2,1,0:T(4,128)S(1)}, u32[]{:S(2)}, u32[]{:S(2)}) collective-permute-start(f32[3,4,4,8]{3,2,1,0:T(4,128)S(1)} %get-tuple-element.236), channel_id=1, source_target_pairs={{4,0},{8,4},{12,8},{16,12},{20,16},{24,20},{28,24},{5,1},{9,5},{13... | collective-permute-start | bytes 4616 | tf_op jit(solution)/shard_map/ppermute | solution.py:43
  198.6 3.9 %collective-permute-start.22 = (f32[3,4,4,8]{3,2,1,0:T(4,128)S(1)}, f32[3,4,4,8]{3,2,1,0:T(4,128)S(1)}, u32[]{:S(2)}, u32[]{:S(2)}) collective-permute-start(f32[3,4,4,8]{3,2,1,0:T(4,128)S(1)} %get-tuple-element.235), channel_id=1, source_target_pairs={{0,4},{4,8},{8,12},{12,16},{16,20},{20,24},{24,28},{1,5},{5,9},{9,... | collective-permute-start | bytes 4616 | tf_op jit(solution)/shard_map/ppermute | solution.py:41
  202.5 6.6 %collective-permute-start.23 = (f32[3,16,4,8]{3,2,1,0:T(4,128)S(1)}, f32[3,16,4,8]{3,2,1,0:T(4,128)S(1)}, u32[]{:S(2)}, u32[]{:S(2)}) collective-permute-start(f32[3,16,4,8]{3,2,1,0:T(4,128)S(1)} %pad_maximum_fusion.14), channel_id=1, source_target_pairs={{2,0},{3,1},{6,4},{7,5},{10,8},{11,9},{14,12},{15,13},{18,16},{19,... | collective-permute-start | bytes 18440 | tf_op jit(solution)/shard_map/ppermute | solution.py:43
  206.9 6.5 %collective-permute-start.24 = (f32[3,16,4,8]{3,2,1,0:T(4,128)S(1)}, f32[3,16,4,8]{3,2,1,0:T(4,128)S(1)}, u32[]{:S(2)}, u32[]{:S(2)}) collective-permute-start(f32[3,16,4,8]{3,2,1,0:T(4,128)S(1)} %pad_maximum_fusion.14), channel_id=1, source_target_pairs={{0,2},{1,3},{4,6},{5,7},{8,10},{9,11},{12,14},{13,15},{16,18},{17,... | collective-permute-start | bytes 18440 | tf_op jit(solution)/shard_map/ppermute | solution.py:41
  213.7 12.6 %collective-permute-start.25 = (f32[3,16,12,4]{3,2,1,0:T(8,128)S(1)}, f32[3,16,12,4]{3,2,1,0:T(8,128)S(1)}, u32[]{:S(2)}, u32[]{:S(2)}) collective-permute-start(f32[3,16,12,4]{3,2,1,0:T(8,128)S(1)} %get-tuple-element.202), channel_id=1, source_target_pairs={{1,0},{3,2},{5,4},{7,6},{9,8},{11,10},{13,12},{15,14},{17,16},{19,... | collective-permute-start | bytes 27656 | tf_op jit(solution)/shard_map/ppermute | solution.py:43
  218.1 12.8 %collective-permute-start.26 = (f32[3,16,12,4]{3,2,1,0:T(8,128)S(1)}, f32[3,16,12,4]{3,2,1,0:T(8,128)S(1)}, u32[]{:S(2)}, u32[]{:S(2)}) collective-permute-start(f32[3,16,12,4]{3,2,1,0:T(8,128)S(1)} %get-tuple-element.203), channel_id=1, source_target_pairs={{0,1},{2,3},{4,5},{6,7},{8,9},{10,11},{12,13},{14,15},{16,17},{18,... | collective-permute-start | bytes 27656 | tf_op jit(solution)/shard_map/ppermute | solution.py:41
  232.9 6.9 %collective-permute-start = (f32[21,1,1,2,8]{0,4,3,2,1:T(8,128)S(1)}, f32[21,1,1,2,8]{0,4,3,2,1:T(8,128)S(1)}, u32[]{:S(2)}, u32[]{:S(2)}) collective-permute-start(f32[21,1,1,2,8]{0,4,3,2,1:T(8,128)S(1)} %get-tuple-element.226), channel_id=1, source_target_pairs={{0,2},{2,4},{4,6},{6,8},{8,10},{10,12},{12,14},{14,16},{16,18},{18... | collective-permute-start | bytes 4040 | tf_op jit(solution)/shard_map/ppermute | solution.py:232
  233.1 9.0 %collective-permute-start.1 = (f32[21,1,1,2,8]{0,4,3,2,1:T(8,128)S(1)}, f32[21,1,1,2,8]{0,4,3,2,1:T(8,128)S(1)}, u32[]{:S(2)}, u32[]{:S(2)}) collective-permute-start(f32[21,1,1,2,8]{0,4,3,2,1:T(8,128)S(1)} %get-tuple-element.225), channel_id=1, source_target_pairs={{0,4},{2,6},{4,8},{6,10},{8,12},{10,14},{12,16},{14,18},{16,20},{1... | collective-permute-start | bytes 4040 | tf_op jit(solution)/shard_map/ppermute | solution.py:232
  236.1 8.4 %collective-permute-start.2 = (f32[21,1,1,2,8]{0,4,3,2,1:T(8,128)S(1)}, f32[21,1,1,2,8]{0,4,3,2,1:T(8,128)S(1)}, u32[]{:S(2)}, u32[]{:S(2)}) collective-permute-start(f32[21,1,1,2,8]{0,4,3,2,1:T(8,128)S(1)} %get-tuple-element.224), channel_id=1, source_target_pairs={{0,6},{2,8},{4,10},{6,12},{8,14},{10,16},{12,18},{14,20},{16,22},{... | collective-permute-start | bytes 4040 | tf_op jit(solution)/shard_map/ppermute | solution.py:232
  238.1 7.7 %collective-permute-start.3 = (f32[21,1,1,2,8]{0,4,3,2,1:T(8,128)S(1)}, f32[21,1,1,2,8]{0,4,3,2,1:T(8,128)S(1)}, u32[]{:S(2)}, u32[]{:S(2)}) collective-permute-start(f32[21,1,1,2,8]{0,4,3,2,1:T(8,128)S(1)} %get-tuple-element.223), channel_id=1, source_target_pairs={{0,8},{2,10},{4,12},{6,14},{8,16},{10,18},{12,20},{14,22},{16,24},... | collective-permute-start | bytes 4040 | tf_op jit(solution)/shard_map/ppermute | solution.py:232
  239.7 6.8 %collective-permute-start.4 = (f32[21,1,1,2,8]{0,4,3,2,1:T(8,128)S(1)}, f32[21,1,1,2,8]{0,4,3,2,1:T(8,128)S(1)}, u32[]{:S(2)}, u32[]{:S(2)}) collective-permute-start(f32[21,1,1,2,8]{0,4,3,2,1:T(8,128)S(1)} %get-tuple-element.222), channel_id=1, source_target_pairs={{0,10},{2,12},{4,14},{6,16},{8,18},{10,20},{12,22},{14,24},{16,26}... | collective-permute-start | bytes 4040 | tf_op jit(solution)/shard_map/ppermute | solution.py:232
  239.8 8.9 %collective-permute-start.5 = (f32[21,1,1,2,8]{0,4,3,2,1:T(8,128)S(1)}, f32[21,1,1,2,8]{0,4,3,2,1:T(8,128)S(1)}, u32[]{:S(2)}, u32[]{:S(2)}) collective-permute-start(f32[21,1,1,2,8]{0,4,3,2,1:T(8,128)S(1)} %get-tuple-element.221), channel_id=1, source_target_pairs={{0,12},{2,14},{4,16},{6,18},{8,20},{10,22},{12,24},{14,26},{16,28}... | collective-permute-start | bytes 4040 | tf_op jit(solution)/shard_map/ppermute | solution.py:232
  242.0 8.7 %collective-permute-start.6 = (f32[21,1,1,2,8]{0,4,3,2,1:T(8,128)S(1)}, f32[21,1,1,2,8]{0,4,3,2,1:T(8,128)S(1)}, u32[]{:S(2)}, u32[]{:S(2)}) collective-permute-start(f32[21,1,1,2,8]{0,4,3,2,1:T(8,128)S(1)} %get-tuple-element.220), channel_id=1, source_target_pairs={{0,14},{2,16},{4,18},{6,20},{8,22},{10,24},{12,26},{14,28},{16,30}... | collective-permute-start | bytes 4040 | tf_op jit(solution)/shard_map/ppermute | solution.py:232
  244.6 6.8 %collective-permute-start.7 = (f32[21,1,1,2,8]{0,4,3,2,1:T(8,128)S(1)}, f32[21,1,1,2,8]{0,4,3,2,1:T(8,128)S(1)}, u32[]{:S(2)}, u32[]{:S(2)}) collective-permute-start(f32[21,1,1,2,8]{0,4,3,2,1:T(8,128)S(1)} %get-tuple-element.219), channel_id=1, source_target_pairs={{0,16},{2,18},{4,20},{6,22},{8,24},{10,26},{12,28},{14,30},{16,0},... | collective-permute-start | bytes 4040 | tf_op jit(solution)/shard_map/ppermute | solution.py:232
  245.8 6.4 %collective-permute-start.8 = (f32[21,1,1,2,8]{0,4,3,2,1:T(8,128)S(1)}, f32[21,1,1,2,8]{0,4,3,2,1:T(8,128)S(1)}, u32[]{:S(2)}, u32[]{:S(2)}) collective-permute-start(f32[21,1,1,2,8]{0,4,3,2,1:T(8,128)S(1)} %get-tuple-element.218), channel_id=1, source_target_pairs={{0,18},{2,20},{4,22},{6,24},{8,26},{10,28},{12,30},{14,0},{16,2},{... | collective-permute-start | bytes 4040 | tf_op jit(solution)/shard_map/ppermute | solution.py:232
  246.6 7.1 %collective-permute-start.9 = (f32[21,1,1,2,8]{0,4,3,2,1:T(8,128)S(1)}, f32[21,1,1,2,8]{0,4,3,2,1:T(8,128)S(1)}, u32[]{:S(2)}, u32[]{:S(2)}) collective-permute-start(f32[21,1,1,2,8]{0,4,3,2,1:T(8,128)S(1)} %get-tuple-element.217), channel_id=1, source_target_pairs={{0,20},{2,22},{4,24},{6,26},{8,28},{10,30},{12,0},{14,2},{16,4},{1... | collective-permute-start | bytes 4040 | tf_op jit(solution)/shard_map/ppermute | solution.py:232
  248.7 7.3 %collective-permute-start.10 = (f32[21,1,1,2,8]{0,4,3,2,1:T(8,128)S(1)}, f32[21,1,1,2,8]{0,4,3,2,1:T(8,128)S(1)}, u32[]{:S(2)}, u32[]{:S(2)}) collective-permute-start(f32[21,1,1,2,8]{0,4,3,2,1:T(8,128)S(1)} %get-tuple-element.216), channel_id=1, source_target_pairs={{0,22},{2,24},{4,26},{6,28},{8,30},{10,0},{12,2},{14,4},{16,6},{18... | collective-permute-start | bytes 4040 | tf_op jit(solution)/shard_map/ppermute | solution.py:232
  250.8 5.2 %collective-permute-start.11 = (f32[21,1,1,2,8]{0,4,3,2,1:T(8,128)S(1)}, f32[21,1,1,2,8]{0,4,3,2,1:T(8,128)S(1)}, u32[]{:S(2)}, u32[]{:S(2)}) collective-permute-start(f32[21,1,1,2,8]{0,4,3,2,1:T(8,128)S(1)} %get-tuple-element.215), channel_id=1, source_target_pairs={{0,24},{2,26},{4,28},{6,30},{8,0},{10,2},{12,4},{14,6},{16,8},{18,... | collective-permute-start | bytes 4040 | tf_op jit(solution)/shard_map/ppermute | solution.py:232
  251.4 4.6 %collective-permute-start.12 = (f32[21,1,1,2,8]{0,4,3,2,1:T(8,128)S(1)}, f32[21,1,1,2,8]{0,4,3,2,1:T(8,128)S(1)}, u32[]{:S(2)}, u32[]{:S(2)}) collective-permute-start(f32[21,1,1,2,8]{0,4,3,2,1:T(8,128)S(1)} %get-tuple-element.214), channel_id=1, source_target_pairs={{0,26},{2,28},{4,30},{6,0},{8,2},{10,4},{12,6},{14,8},{16,10},{18,... | collective-permute-start | bytes 4040 | tf_op jit(solution)/shard_map/ppermute | solution.py:232
  252.2 3.9 %collective-permute-start.13 = (f32[21,1,1,2,8]{0,4,3,2,1:T(8,128)S(1)}, f32[21,1,1,2,8]{0,4,3,2,1:T(8,128)S(1)}, u32[]{:S(2)}, u32[]{:S(2)}) collective-permute-start(f32[21,1,1,2,8]{0,4,3,2,1:T(8,128)S(1)} %get-tuple-element.213), channel_id=1, source_target_pairs={{0,28},{2,30},{4,0},{6,2},{8,4},{10,6},{12,8},{14,10},{16,12},{18,... | collective-permute-start | bytes 4040 | tf_op jit(solution)/shard_map/ppermute | solution.py:232
  253.7 3.7 %collective-permute-start.14 = (f32[21,1,1,2,8]{0,4,3,2,1:T(8,128)S(1)}, f32[21,1,1,2,8]{0,4,3,2,1:T(8,128)S(1)}, u32[]{:S(2)}, u32[]{:S(2)}) collective-permute-start(f32[21,1,1,2,8]{0,4,3,2,1:T(8,128)S(1)} %get-tuple-element.212), channel_id=1, source_target_pairs={{0,30},{2,0},{4,2},{6,4},{8,6},{10,8},{12,10},{14,12},{16,14},{18,... | collective-permute-start | bytes 4040 | tf_op jit(solution)/shard_map/ppermute | solution.py:232
  257.9 1.7 copy-start
  259.6 0.9 copy-start.2
  260.8 2.6 collective-permute-start.27
  262.1 3.4 %collective-permute-start.28 = (f32[6,4,4,8]{3,2,1,0:T(4,128)S(1)}, f32[6,4,4,8]{3,2,1,0:T(4,128)S(1)}, u32[]{:S(2)}, u32[]{:S(2)}) collective-permute-start(f32[6,4,4,8]{3,2,1,0:T(4,128)S(1)} %get-tuple-element.228), channel_id=1, source_target_pairs={{4,0},{8,4},{12,8},{16,12},{20,16},{24,20},{28,24},{5,1},{9,5},{13... | collective-permute-start | bytes 9224 | tf_op jit(solution)/shard_map/ppermute | solution.py:43
  265.5 7.9 %collective-permute-start.29 = (f32[6,16,4,8]{3,2,1,0:T(4,128)S(1)}, f32[6,16,4,8]{3,2,1,0:T(4,128)S(1)}, u32[]{:S(2)}, u32[]{:S(2)}) collective-permute-start(f32[6,16,4,8]{3,2,1,0:T(4,128)S(1)} %pad_maximum_fusion.12), channel_id=1, source_target_pairs={{0,2},{1,3},{4,6},{5,7},{8,10},{9,11},{12,14},{13,15},{16,18},{17,... | collective-permute-start | bytes 36872 | tf_op jit(solution)/shard_map/ppermute | solution.py:41
  266.8 8.3 %collective-permute-start.30 = (f32[6,16,4,8]{3,2,1,0:T(4,128)S(1)}, f32[6,16,4,8]{3,2,1,0:T(4,128)S(1)}, u32[]{:S(2)}, u32[]{:S(2)}) collective-permute-start(f32[6,16,4,8]{3,2,1,0:T(4,128)S(1)} %pad_maximum_fusion.12), channel_id=1, source_target_pairs={{2,0},{3,1},{6,4},{7,5},{10,8},{11,9},{14,12},{15,13},{18,16},{19,... | collective-permute-start | bytes 36872 | tf_op jit(solution)/shard_map/ppermute | solution.py:43
  276.1 7.9 %collective-permute-start.31 = (f32[6,16,12,4]{1,3,2,0:T(4,128)S(1)}, f32[6,16,12,4]{1,3,2,0:T(4,128)S(1)}, u32[]{:S(2)}, u32[]{:S(2)}) collective-permute-start(f32[6,16,12,4]{1,3,2,0:T(4,128)S(1)} %copy.178), channel_id=1, source_target_pairs={{0,1},{2,3},{4,5},{6,7},{8,9},{10,11},{12,13},{14,15},{16,17},{18,... | collective-permute-start | bytes 55304 | tf_op jit(solution)/shard_map/ppermute | solution.py:41
  277.9 8.4 %collective-permute-start.32 = (f32[6,16,12,4]{1,3,2,0:T(4,128)S(1)}, f32[6,16,12,4]{1,3,2,0:T(4,128)S(1)}, u32[]{:S(2)}, u32[]{:S(2)}) collective-permute-start(f32[6,16,12,4]{1,3,2,0:T(4,128)S(1)} %copy.179), channel_id=1, source_target_pairs={{1,0},{3,2},{5,4},{7,6},{9,8},{11,10},{13,12},{15,14},{17,16},{19,... | collective-permute-start | bytes 55304 | tf_op jit(solution)/shard_map/ppermute | solution.py:43
  288.3 34.6 %copy-start.1 = (f32[3,8,4,8]{3,2,1,0:T(4,128)}, f32[3,8,4,8]{3,2,1,0:T(4,128)S(1)}, u32[]{:S(2)}) copy-start(f32[3,8,4,8]{3,2,1,0:T(4,128)S(1)} %divide_add_fusion) | copy-start | bytes 9220
  288.4 4.4 %collective-permute-start.33 = (f32[3,4,4,8]{3,2,1,0:T(4,128)S(1)}, f32[3,4,4,8]{3,2,1,0:T(4,128)S(1)}, u32[]{:S(2)}, u32[]{:S(2)}) collective-permute-start(f32[3,4,4,8]{3,2,1,0:T(4,128)S(1)} %get-tuple-element.234), channel_id=1, source_target_pairs={{4,0},{8,4},{12,8},{16,12},{20,16},{24,20},{28,24},{5,1},{9,5},{13... | collective-permute-start | bytes 4616 | tf_op jit(solution)/shard_map/ppermute | solution.py:43
  289.7 3.9 %collective-permute-start.34 = (f32[3,4,4,8]{3,2,1,0:T(4,128)S(1)}, f32[3,4,4,8]{3,2,1,0:T(4,128)S(1)}, u32[]{:S(2)}, u32[]{:S(2)}) collective-permute-start(f32[3,4,4,8]{3,2,1,0:T(4,128)S(1)} %get-tuple-element.233), channel_id=1, source_target_pairs={{0,4},{4,8},{8,12},{12,16},{16,20},{20,24},{24,28},{1,5},{5,9},{9,... | collective-permute-start | bytes 4616 | tf_op jit(solution)/shard_map/ppermute | solution.py:41
  293.6 6.9 %collective-permute-start.35 = (f32[3,16,4,8]{3,2,1,0:T(4,128)S(1)}, f32[3,16,4,8]{3,2,1,0:T(4,128)S(1)}, u32[]{:S(2)}, u32[]{:S(2)}) collective-permute-start(f32[3,16,4,8]{3,2,1,0:T(4,128)S(1)} %pad_maximum_fusion.15), channel_id=1, source_target_pairs={{2,0},{3,1},{6,4},{7,5},{10,8},{11,9},{14,12},{15,13},{18,16},{19,... | collective-permute-start | bytes 18440 | tf_op jit(solution)/shard_map/ppermute | solution.py:43
  298.3 7.0 %collective-permute-start.36 = (f32[3,16,4,8]{3,2,1,0:T(4,128)S(1)}, f32[3,16,4,8]{3,2,1,0:T(4,128)S(1)}, u32[]{:S(2)}, u32[]{:S(2)}) collective-permute-start(f32[3,16,4,8]{3,2,1,0:T(4,128)S(1)} %pad_maximum_fusion.15), channel_id=1, source_target_pairs={{0,2},{1,3},{4,6},{5,7},{8,10},{9,11},{12,14},{13,15},{16,18},{17,... | collective-permute-start | bytes 18440 | tf_op jit(solution)/shard_map/ppermute | solution.py:41
  305.5 13.3 %collective-permute-start.37 = (f32[3,16,12,4]{3,2,1,0:T(8,128)S(1)}, f32[3,16,12,4]{3,2,1,0:T(8,128)S(1)}, u32[]{:S(2)}, u32[]{:S(2)}) collective-permute-start(f32[3,16,12,4]{3,2,1,0:T(8,128)S(1)} %get-tuple-element.200), channel_id=1, source_target_pairs={{1,0},{3,2},{5,4},{7,6},{9,8},{11,10},{13,12},{15,14},{17,16},{19,... | collective-permute-start | bytes 27656 | tf_op jit(solution)/shard_map/ppermute | solution.py:43
  309.9 13.0 %collective-permute-start.38 = (f32[3,16,12,4]{3,2,1,0:T(8,128)S(1)}, f32[3,16,12,4]{3,2,1,0:T(8,128)S(1)}, u32[]{:S(2)}, u32[]{:S(2)}) collective-permute-start(f32[3,16,12,4]{3,2,1,0:T(8,128)S(1)} %get-tuple-element.201), channel_id=1, source_target_pairs={{0,1},{2,3},{4,5},{6,7},{8,9},{10,11},{12,13},{14,15},{16,17},{18,... | collective-permute-start | bytes 27656 | tf_op jit(solution)/shard_map/ppermute | solution.py:41
  324.1 0.6 copy-start.9
Sparse Core Ops, SparseCore 0:
  166.1 14.5 reduce-scatter.1
